TPU v7x, 32 devices: a whole 2x2x4 slice. The times are simulated.
32 devices in a mesh: row: 4 (over x, core), col: 8 (over z, y).
Axes of the slice: x: 2, y: 2, z: 4, core: 2. Of those that a mesh axis runs over, the one named last changes fastest.
Arguments:
- node_features: bfloat16 [4096, 256], P(('row', 'col')), may hold values from -6 to 6
- layer_weight: bfloat16 [256, 256], replicated, may hold values from -0.375 to 0.375
- output_grad: bfloat16 [4096, 256], P(('row', 'col')), may hold values from -6 to 6
- block_values: bfloat16 [4, 8, 24, 128, 128], P('row', 'col'), may hold values from -0.15625 to 0.15625
- block_position: int32 [4, 8, 24], P('row', 'col'), may hold values from 0 to 31, as said below
- tile_count: int32 [4, 8], P('row', 'col'), may hold values from 6 to 24, as said below
Outputs:
- node_output: bfloat16 [4096, 256], P(('row', 'col'))
- input_grad: bfloat16 [4096, 256], P(('row', 'col'))
- weight_grad: float32 [256, 256], replicated
Inputs may be any that keep to these rules, and one draw needn't show every extreme that they name: Tile (r, c) uses its slots 0 to tile_count[r, c] - 1; in every draw some tile uses all 24 slots. `block_position`: the slots of a tile hold distinct positions in increasing order.
All inputs are finite; a program needn't handle non-finite values.
Results may differ from a plain program's by a relative error of at most 0.02.
Values may be sent and summed in bfloat16 or wider, within the bound.
A program may use at most 64 MiB of HBM per device.

v0:
```python
import functools
import math

import jax
import jax.numpy as jnp
from jax import lax
from jax.experimental import pallas as pl
from jax.experimental.pallas import tpu as pltpu
from jax.sharding import PartitionSpec as P

MESH = pl.DeviceIdType.MESH
F32 = jnp.float32
BF16 = jnp.bfloat16


def repeat(steps, step):
    if len(steps) <= 8:
        for d in steps:
            step(d)
    else:

        def one(d, unused):
            step(d)
            return unused

        lax.fori_loop(min(steps), max(steps) + 1, one, 0)


def split_dot(left, right, dims):
    high = left.astype(BF16)
    low = (left - high.astype(F32)).astype(BF16)
    first = lax.dot_general(high, right, dims, preferred_element_type=F32)
    return first + lax.dot_general(low, right, dims, preferred_element_type=F32)


def kernel(
    rows,
    cols,
    position_hbm,
    count_hbm,
    x_hbm,
    w_hbm,
    og_hbm,
    values_hbm,
    out_ref,
    ig_ref,
    wg_ref,
    position,
    count,
    values,
    w_ref,
    og_ref,
    xg,
    tile,
    tile_t,
    mate_part,
    mate_in,
    part,
    part_in,
    up,
    acc,
    pc,
    pc_in,
    term,
    w1_in,
    own,
    w2_in,
    small,
    w3_in,
    w4_in,
    sem_v,
    sem_x,
    sem_y,
    sem_z,
    sem_u,
    sem_f,
    sem_c,
    sem_w1,
    sem_w2,
    sem_w3,
    sem_w4,
):
    nodes, width = x_hbm.shape
    slots, block = values_hbm.shape[0], values_hbm.shape[1]
    col_blocks = rows
    my_row = lax.axis_index("row")
    my_col = lax.axis_index("col")
    size = {"row": rows, "col": cols}
    me = {"row": my_row, "col": my_col}
    half = cols // 2
    my_high = my_col // 2
    my_low = lax.rem(my_col, 2)
    mate = my_high * 2 + 1 - my_low
    others = [half // 2] + [d for d in range(1, half) if d != half // 2]
    pieces = [pl.ds(p * nodes // 2, nodes // 2) for p in range(2)]
    count_pieces = len(pieces)
    row_steps = list(range(1, rows))
    col_steps = list(range(1, cols))

    def ahead(axis, d):
        return lax.rem(me[axis] + d, size[axis])

    def behind(axis, d):
        return lax.rem(me[axis] + size[axis] - d, size[axis])

    def high_ahead(d):
        return lax.rem(my_high + d, half)

    def high_behind(d):
        return lax.rem(my_high + half - d, half)

    def move(sem, index, src, dst, **target):
        return pltpu.make_async_remote_copy(
            src_ref=src,
            dst_ref=dst,
            send_sem=sem.at[0, index],
            recv_sem=sem.at[1, index],
            device_id=target,
            device_id_type=MESH,
        )

    def send(axis, sem, d, src, dst):
        return move(sem, d - 1, src, dst, **{axis: ahead(axis, d)})

    load = pltpu.make_async_copy(values_hbm, values.at[pl.ds(0, slots)], sem_v.at[0])
    load_x = pltpu.make_async_copy(x_hbm, xg.at[my_row], sem_v.at[1])
    load_w = pltpu.make_async_copy(w_hbm, w_ref, sem_v.at[2])
    load_og = pltpu.make_async_copy(og_hbm, og_ref, sem_v.at[3])
    load_position = pltpu.make_async_copy(position_hbm, position, sem_v.at[4])
    load_count = pltpu.make_async_copy(count_hbm, count, sem_v.at[5])
    for one in (load_position, load_count, load, load_x, load_w, load_og):
        one.start()

    barrier = pltpu.get_barrier_semaphore()

    def greet(**target):
        pl.semaphore_signal(barrier, inc=1, device_id=target, device_id_type=MESH)

    repeat(others, lambda d: greet(col=high_ahead(d) * 2 + my_low))
    greet(col=mate)
    repeat(row_steps, lambda d: greet(row=ahead("row", d)))
    values[slots] = jnp.zeros((block, block), BF16)
    pl.semaphore_wait(barrier, rows + half - 1)

    repeat(row_steps, lambda d: send("row", sem_x, d, x_hbm, xg.at[my_row]).start())

    load_position.wait()
    load_count.wait()
    load.wait()
    live_count = count[0, 0]

    def build(q, pointer):
        for k in range(col_blocks):
            here = position[jnp.minimum(pointer, slots - 1)]
            live = (here == q * col_blocks + k) & (pointer < live_count)
            slot = jnp.where(live, pointer, slots)
            tile[q, :, pl.ds(k * block, block)] = values[slot]
            pointer = pointer + live.astype(jnp.int32)
        return pointer

    if cols <= 8:
        pointer = jnp.int32(0)
        for q in range(cols):
            pointer = build(q, pointer)
    else:
        lax.fori_loop(0, cols, build, jnp.int32(0))

    load_x.wait()

    def from_row(d):
        slot = xg.at[behind("row", d)]
        send("row", sem_x, d, slot, slot).wait_recv()

    repeat(row_steps, from_row)
    panel = xg[...].reshape(rows * nodes, width)

    def to_mate(d):
        high = high_ahead(d)
        product = jnp.dot(tile[high * 2 + 1 - my_low], panel, preferred_element_type=F32)
        mate_part[high] = product.astype(BF16)
        for p, some in enumerate(pieces):
            index = d * count_pieces + p
            move(sem_y, index, mate_part.at[high, some], mate_in.at[high, some], col=mate).start()

    repeat(others, to_mate)
    to_mate(0)

    def from_mate(d, take):
        high = high_ahead(d)
        own[...] = jnp.dot(tile[high * 2 + my_low], panel, preferred_element_type=F32)
        for p, some in enumerate(pieces):
            slot = mate_in.at[high, some]
            move(sem_y, d * count_pieces + p, slot, slot, col=mate).wait_recv()
            take(p, some, own[some] + mate_in[high, some].astype(F32))

    def to_high(d):
        high = high_ahead(d)

        def take(p, some, total):
            part[high, some] = total.astype(BF16)
            move(
                sem_z,
                (d - 1) * count_pieces + p,
                part.at[high, some],
                part_in.at[my_high, some],
                col=high * 2 + my_low,
            ).start()

        from_mate(d, take)

    def keep(p, some, total):
        own[some] = total

    repeat(others, to_high)
    from_mate(0, keep)

    def turn(q):
        for k in range(col_blocks):
            tile_t[q, pl.ds(k * block, block), :] = tile[q, :, pl.ds(k * block, block)].T

    repeat(list(range(cols)), turn)

    def add_part(d):
        high = high_behind(d)
        for p, some in enumerate(pieces):
            slot = part_in.at[high, some]
            index = (d - 1) * count_pieces + p
            move(sem_z, index, slot, slot, col=high * 2 + my_low).wait_recv()
        own[...] += part_in[high].astype(F32)

    load_w.wait()
    load_og.wait()
    repeat(others, add_part)
    mixed = own[...]
    pre = split_dot(mixed, w_ref[...], (((1,), (0,)), ((), ())))
    decay = jnp.exp(jnp.minimum(pre, 0.0))
    slope = jnp.where(pre > 0, 1.0, decay)
    up[my_col] = (og_ref[...].astype(F32) * slope).astype(BF16)

    def up_high(d):
        for p, some in enumerate(pieces):
            mine = up.at[my_col, some]
            index = (d - 1) * count_pieces + p
            move(sem_u, index, mine, mine, col=high_ahead(d) * 2 + my_low).start()

    for p, some in enumerate(pieces):
        move(sem_f, p, up.at[my_col, some], up.at[my_col, some], col=mate).start()
    repeat(others, up_high)
    out_ref[...] = jnp.where(pre > 0, pre, decay - 1.0).astype(BF16)

    scale = 1.0 / math.sqrt(nodes * rows * cols)
    share = width // rows
    over_nodes = (((0,), (0,)), ((), ()))
    upstream = up[my_col]
    term[...] = (split_dot(mixed, upstream, over_nodes) * scale).reshape(rows, share, width).astype(BF16)
    repeat(
        row_steps,
        lambda d: send("row", sem_w1, d, term.at[ahead("row", d)], w1_in.at[my_row]).start(),
    )

    acc[...] = jnp.dot(tile_t[my_col], upstream, preferred_element_type=F32)

    def back(source):
        acc[...] += jnp.dot(tile_t[source], up[source], preferred_element_type=F32)

    def back_high(d):
        source = high_behind(d) * 2 + my_low
        for p, some in enumerate(pieces):
            slot = up.at[source, some]
            move(sem_u, (d - 1) * count_pieces + p, slot, slot, col=source).wait_recv()
            move(sem_f, d * count_pieces + p, slot, slot, col=mate).start()
        back(source)

    def back_mate(d):
        source = high_behind(d) * 2 + 1 - my_low
        for p, some in enumerate(pieces):
            slot = up.at[source, some]
            move(sem_f, d * count_pieces + p, slot, slot, col=mate).wait_recv()
        back(source)

    back_mate(0)

    small[...] = term[my_row].astype(F32)

    def add_w1(d):
        slot = w1_in.at[behind("row", d)]
        send("row", sem_w1, d, slot, slot).wait_recv()
        small[...] += w1_in[behind("row", d)].astype(F32)

    repeat(row_steps, add_w1)
    piece = share // cols
    scattered = piece >= 8 and piece % 8 == 0
    if scattered:

        def send_w2(d):
            src = small.at[pl.ds(pl.multiple_of(ahead("col", d) * piece, piece), piece)]
            send("col", sem_w2, d, src, w2_in.at[my_col]).start()
    else:

        def send_w2(d):
            send("col", sem_w2, d, small, w2_in.at[my_col]).start()

    repeat(col_steps, send_w2)

    def w2_wait(d):
        slot = w2_in.at[behind("col", d)]
        send("col", sem_w2, d, slot, slot).wait_recv()

    repeat(others, back_high)
    repeat(col_steps, w2_wait)
    if scattered:
        w2_in[my_col] = small[pl.ds(pl.multiple_of(my_col * piece, piece), piece), :]
        w3_in[my_col] = jnp.sum(w2_in[...], axis=0)
        repeat(
            col_steps,
            lambda d: send("col", sem_w3, d, w3_in.at[my_col], w3_in.at[my_col]).start(),
        )
    else:
        w2_in[my_col] = small[...]
        w4_in[my_row] = jnp.sum(w2_in[...], axis=0).astype(BF16)

    repeat(others, back_mate)

    def scatter_cols(d):
        to = ahead("row", d)
        pc[to] = acc[pl.ds(pl.multiple_of(to * nodes, nodes), nodes), :].astype(BF16)
        send("row", sem_c, d, pc.at[to], pc_in.at[my_row]).start()

    repeat(row_steps, scatter_cols)

    if scattered:

        def w3_wait(d):
            slot = w3_in.at[behind("col", d)]
            send("col", sem_w3, d, slot, slot).wait_recv()

        repeat(col_steps, w3_wait)
        w4_in[my_row] = w3_in[...].reshape(share, width).astype(BF16)
    repeat(
        row_steps, lambda d: send("row", sem_w4, d, w4_in.at[my_row], w4_in.at[my_row]).start()
    )

    own[...] = acc[pl.ds(pl.multiple_of(my_row * nodes, nodes), nodes), :]

    def add_pc(d):
        slot = pc_in.at[behind("row", d)]
        send("row", sem_c, d, slot, slot).wait_recv()
        own[...] += pc_in[behind("row", d)].astype(F32)

    repeat(row_steps, add_pc)
    ig_ref[...] = split_dot(own[...], w_ref[...], (((1,), (1,)), ((), ()))).astype(BF16)

    def row_sent(d):
        send("row", sem_x, d, x_hbm, xg.at[my_row]).wait_send()
        send("row", sem_w1, d, term.at[my_row], w1_in.at[my_row]).wait_send()
        send("row", sem_c, d, pc.at[my_row], pc_in.at[my_row]).wait_send()
        send("row", sem_w4, d, w4_in.at[my_row], w4_in.at[my_row]).wait_send()

    def col_sent(d):
        if scattered:
            send("col", sem_w2, d, small.at[pl.ds(0, piece)], w2_in.at[my_col]).wait_send()
            send("col", sem_w3, d, w3_in.at[my_col], w3_in.at[my_col]).wait_send()
        else:
            send("col", sem_w2, d, small, w2_in.at[my_col]).wait_send()

    def mate_sent(d):
        for p, some in enumerate(pieces):
            mine = up.at[my_col, some]
            gone = mate_part.at[0, some]
            move(sem_y, d * count_pieces + p, gone, mate_in.at[0, some], col=mate).wait_send()
            move(sem_f, d * count_pieces + p, mine, mine, col=mate).wait_send()

    def high_sent(d):
        for p, some in enumerate(pieces):
            mine = up.at[my_col, some]
            gone = part.at[0, some]
            index = (d - 1) * count_pieces + p
            move(sem_z, index, gone, part_in.at[0, some], col=mate).wait_send()
            move(sem_u, index, mine, mine, col=mate).wait_send()

    repeat(list(range(half)), mate_sent)
    repeat(list(range(1, half)), high_sent)
    repeat(col_steps, col_sent)

    def w4_wait(d):
        slot = w4_in.at[behind("row", d)]
        send("row", sem_w4, d, slot, slot).wait_recv()

    repeat(row_steps, w4_wait)
    wg_ref[...] = w4_in[...].reshape(width, width).astype(F32)
    repeat(row_steps, row_sent)


def finish(out_ref, ig_ref, wg_ref, out_hbm, ig_hbm, wg_hbm, sem):
    trio = ((out_ref, out_hbm), (ig_ref, ig_hbm), (wg_ref, wg_hbm))
    copies = [pltpu.make_async_copy(a, b, sem.at[i]) for i, (a, b) in enumerate(trio)]
    for copy in copies:
        copy.start()
    for copy in copies:
        copy.wait()


def body(node_features, layer_weight, output_grad, block_values, block_position, tile_count):
    rows, cols = lax.axis_size("row"), lax.axis_size("col")
    nodes, width = node_features.shape
    slots, block = block_values.shape[2], block_values.shape[3]
    assert nodes == block
    share = width // rows
    piece = share // cols
    if not (piece >= 8 and piece % 8 == 0):
        piece = share
    place = pl.BlockSpec(memory_space=pl.ANY)
    inside = pl.BlockSpec(memory_space=pltpu.VMEM)
    half = cols // 2
    assert cols == 2 * half
    dma = pltpu.SemaphoreType.DMA
    shapes = (
        jax.ShapeDtypeStruct((nodes, width), BF16),
        jax.ShapeDtypeStruct((nodes, width), BF16),
        jax.ShapeDtypeStruct((width, width), F32),
    )
    results = pl.pallas_call(
        functools.partial(kernel, rows, cols),
        out_shape=(
            pltpu.VMEM((nodes, width), BF16),
            pltpu.VMEM((nodes, width), BF16),
            pltpu.VMEM((width, width), F32),
        ),
        in_specs=[place, place, place, place, place, place],
        out_specs=(inside, inside, inside),
        scratch_shapes=[
            pltpu.SMEM((slots,), jnp.int32),
            pltpu.SMEM((1, 1), jnp.int32),
            pltpu.VMEM((slots + 1, block, block), BF16),
            pltpu.VMEM((width, width), BF16),
            pltpu.VMEM((nodes, width), BF16),
            pltpu.VMEM((rows, nodes, width), BF16),
            pltpu.VMEM((cols, nodes, rows * nodes), BF16),
            pltpu.VMEM((cols, rows * nodes, nodes), BF16),
            pltpu.VMEM((half, nodes, width), BF16),
            pltpu.VMEM((half, nodes, width), BF16),
            pltpu.VMEM((half, nodes, width), BF16),
            pltpu.VMEM((half, nodes, width), BF16),
            pltpu.VMEM((cols, nodes, width), BF16),
            pltpu.VMEM((rows * nodes, width), F32),
            pltpu.VMEM((rows, nodes, width), BF16),
            pltpu.VMEM((rows, nodes, width), BF16),
            pltpu.VMEM((rows, share, width), BF16),
            pltpu.VMEM((rows, share, width), BF16),
            pltpu.VMEM((nodes, width), F32),
            pltpu.VMEM((cols, piece, width), F32),
            pltpu.VMEM((share, width), F32),
            pltpu.VMEM((cols, piece, width), F32),
            pltpu.VMEM((rows, share, width), BF16),
            dma((7,)),
            dma((2, rows - 1)),
            dma((2, half * 2)),
            dma((2, (half - 1) * 2)),
            dma((2, (half - 1) * 2)),
            dma((2, half * 2)),
            dma((2, rows - 1)),
            dma((2, rows - 1)),
            dma((2, cols - 1)),
            dma((2, cols - 1)),
            dma((2, rows - 1)),
        ],
        compiler_params=pltpu.CompilerParams(collective_id=0, has_side_effects=True),
    )(
        block_position.reshape(slots),
        tile_count,
        node_features,
        layer_weight,
        output_grad,
        block_values.reshape(slots, block, block),
    )
    return pl.pallas_call(
        finish,
        out_shape=shapes,
        in_specs=[inside] * 3,
        out_specs=(place,) * 3,
        scratch_shapes=[
            dma((3,)),
        ],
        compiler_params=pltpu.CompilerParams(vmem_limit_bytes=4 << 20),
    )(*results)


def solution(mesh):
    in_specs = (
        P(("row", "col"), None),
        P(),
        P(("row", "col"), None),
        P("row", "col", None, None, None),
        P("row", "col", None),
        P("row", "col"),
    )
    out_specs = (P(("row", "col"), None), P(("row", "col"), None), P())
    return jax.shard_map(body, mesh=mesh, in_specs=in_specs, out_specs=out_specs, check_vma=False)
```

profile of v0, /device:TPU:0, one launch (start us, length us, event | category | flops | bytes accessed | tf_op | source)
XLA Modules:
  0.0 40.0 jit_solution(7218036752408726701)
XLA Ops:
  1.3 38.0 %shard_map.85 = (bf16[128,256]{1,0:T(8,128)(2,1)S(1)}, bf16[128,256]{1,0:T(8,128)(2,1)S(1)}, f32[256,256]{1,0:T(8,128)S(1)}) custom-call(s32[24]{0:T(128)} %bitcast.3, s32[1,1]{1,0:T(1,128)S(6)} %copy.9.count_hbm, bf16[128,256]{1,0:T(8,128)(2,1)} %x_hbm.1, bf16[256,256]{1,0:T(8,128)(2,1)} %w_hbm.1, bf16[128,256]{1,0:T(8,128)(2,1)} %og_hbm.1, ...), custom_call_target="tpu_custom_call" | custom-call | tf_op jit(solution)/shard_map/pallas_call | solution.py:422
  39.3 0.8 %shard_map.86 = (bf16[128,256]{1,0:T(8,128)(2,1)}, bf16[128,256]{1,0:T(8,128)(2,1)}, f32[256,256]{1,0:T(8,128)}) custom-call(bf16[128,256]{1,0:T(8,128)(2,1)S(1)} %get-tuple-element.6.out_ref, bf16[128,256]{1,0:T(8,128)(2,1)S(1)} %get-tuple-element.7.ig_ref, f32[256,256]{1,0:T(8,128)S(1)} %get-tuple-element.8.wg_ref), custom_call_target="tpu_custom_call" | custom-call | tf_op jit(solution)/shard_map/pallas_call | solution.py:476
where the time goes:
time: 40.2 us; the launch traced here: 40 us
  Pallas kernels  38.7 us (96%)
  between operations  1.29 us (3%)
    pallas_call x1, Pallas kernels, body(): pl.pallas_call(functools.partial(kernel, rows, cols), out_shape=(pltpu.VM...  38 us

commit v1 on v0

v1 whole, which is shorter than its diff:
```python
import functools
import math

import jax
import jax.numpy as jnp
from jax import lax
from jax.experimental import pallas as pl
from jax.experimental.pallas import tpu as pltpu
from jax.sharding import PartitionSpec as P

MESH = pl.DeviceIdType.MESH
F32 = jnp.float32
BF16 = jnp.bfloat16
PARTS = 2
FEATS = 2


def repeat(steps, step):
    if len(steps) <= 8:
        for d in steps:
            step(d)
    elif len(steps) > 0:

        def one(d, unused):
            step(d)
            return unused

        lax.fori_loop(min(steps), max(steps) + 1, one, 0)


def split_dot(left, right, dims):
    high = left.astype(BF16)
    low = (left - high.astype(F32)).astype(BF16)
    first = lax.dot_general(high, right, dims, preferred_element_type=F32)
    return first + lax.dot_general(low, right, dims, preferred_element_type=F32)


def counts(rows, cols):
    half = cols // 2
    return {
        "load": 6,
        "x_mate": 1,
        "x_lead": 1,
        "x_rest": 1,
        "x_pass": 1,
        "ry": PARTS * half,
        "rz": PARTS,
        "gz": (1 + FEATS) * (half - 1),
        "gy": 1 + FEATS,
        "c_mate": FEATS,
        "c_pre": FEATS,
        "c_rest": FEATS,
        "c_lead": FEATS,
        "w": 3,
        "s_x": 1,
        "s_ry": 1,
        "s_rz": 1,
        "s_gz": 1,
        "s_gy": 1,
        "s_c": 1,
        "s_w": 3,
    }


def kernel(
    rows,
    cols,
    position_hbm,
    count_hbm,
    x_hbm,
    w_hbm,
    og_hbm,
    values_hbm,
    out_ref,
    ig_ref,
    wg_ref,
    position,
    count,
    values,
    w_ref,
    og_ref,
    xg,
    tile,
    tile_t,
    mate_part,
    mate_in,
    own,
    part,
    part_in,
    keep,
    up,
    acc,
    term_sum,
    term,
    w1_in,
    w2_in,
    w3_in,
    pc,
    pc_mate,
    pre_in,
    rest_in,
    lead_in,
    sems,
):
    scope = jax.named_scope
    nodes, width = x_hbm.shape
    slots, block = values_hbm.shape[0], values_hbm.shape[1]
    col_blocks = rows
    my_row = lax.axis_index("row")
    my_col = lax.axis_index("col")
    half = cols // 2
    exts = rows // 2
    high = my_col // 2
    low = lax.rem(my_col, 2)
    mate = high * 2 + 1 - low
    ext = my_row // 2
    core = lax.rem(my_row, 2)
    core_mate = ext * 2 + 1 - core
    plane = 2 * rows
    my_spot = my_row * 2 + low
    sub = nodes // PARTS
    fw = width // FEATS
    lead = nodes // 2
    rest = nodes - lead
    group = min(half, 4)
    groups = half // group
    others = [half // 2] + [d for d in range(1, half) if d != half // 2]
    ext_steps = list(range(1, exts))
    lead_rows, rest_rows = pl.ds(0, lead), pl.ds(lead, rest)

    base, at = {}, 0
    for name, size in counts(rows, cols).items():
        base[name] = at
        at += size

    def sem(name, index=0):
        return sems.at[base[name] + index]

    def high_ahead(d):
        return lax.rem(high + d, half)

    def high_behind(d):
        return lax.rem(high + half - d, half)

    def ext_ahead(d):
        return lax.rem(ext + d, exts)

    def ext_behind(d):
        return lax.rem(ext + exts - d, exts)

    def spot_ahead(d):
        return lax.rem(my_spot + d, plane)

    def move(src, dst, sent, got, **target):
        return pltpu.make_async_remote_copy(
            src_ref=src,
            dst_ref=dst,
            send_sem=sent,
            recv_sem=got,
            device_id=target,
            device_id_type=MESH,
        )

    def arrived(ref, got):
        move(ref, ref, sem("s_x"), got, col=mate).wait_recv()

    def gone(ref, sent):
        move(ref, ref, sent, sem("x_mate"), col=mate).wait_send()

    load = pltpu.make_async_copy(values_hbm, values.at[pl.ds(0, slots)], sem("load", 0))
    load_x = pltpu.make_async_copy(x_hbm, xg.at[my_row], sem("load", 1))
    load_w = pltpu.make_async_copy(w_hbm, w_ref, sem("load", 2))
    load_og = pltpu.make_async_copy(og_hbm, og_ref, sem("load", 3))
    load_position = pltpu.make_async_copy(position_hbm, position, sem("load", 4))
    load_count = pltpu.make_async_copy(count_hbm, count, sem("load", 5))
    for one in (load_x, load_position, load_count, load, load_w, load_og):
        one.start()

    barrier = pltpu.get_barrier_semaphore()

    def greet(**target):
        pl.semaphore_signal(barrier, inc=1, device_id=target, device_id_type=MESH)

    repeat(others, lambda d: greet(col=high_ahead(d) * 2 + low))

    def greet_spot(d):
        spot = spot_ahead(d)
        greet(row=spot // 2, col=high * 2 + lax.rem(spot, 2))

    repeat(list(range(1, plane)), greet_spot)
    values[slots] = jnp.zeros((block, block), BF16)
    load_x.wait()
    with scope("bar"):
        pl.semaphore_wait(barrier, plane - 1 + half - 1)

    mine = xg.at[my_row]

    def x_lead(d):
        move(
            mine.at[lead_rows], xg.at[my_row, lead_rows], sem("s_x"), sem("x_lead"),
            row=ext_ahead(d) * 2 + core,
        ).start()

    def x_rest(d):
        for to in (core, 1 - core):
            move(
                mine.at[rest_rows], xg.at[my_row, rest_rows], sem("s_x"), sem("x_rest"),
                row=ext_ahead(d) * 2 + to,
            ).start()

    repeat(ext_steps, x_lead)
    move(mine, mine, sem("s_x"), sem("x_mate"), row=core_mate).start()
    repeat(ext_steps, x_rest)

    with scope("load"):
        load_position.wait()
        load_count.wait()
        load.wait()
    live_count = count[0, 0]

    def build(q, y, z, pointer):
        for k in range(col_blocks):
            here = position[jnp.minimum(pointer, slots - 1)]
            live = (here == q * col_blocks + k) & (pointer < live_count)
            value = values[jnp.where(live, pointer, slots)]
            for p in range(PARTS):
                tile[p, y, z, :, pl.ds(k * block, block)] = value[p * sub : (p + 1) * sub, :]
            pointer = pointer + live.astype(jnp.int32)
        return pointer

    with scope("build"):
        if cols <= 8:
            pointer = jnp.int32(0)
            for q in range(cols):
                pointer = build(q, q % 2, q // 2, pointer)
        else:

            def build_pair(z, pointer):
                for y in range(2):
                    pointer = build(z * 2 + y, y, z, pointer)
                return pointer

            lax.fori_loop(0, half, build_pair, jnp.int32(0))

    with scope("x_lead"):
        arrived(xg.at[pl.ds(0, exts - 1), lead_rows], sem("x_lead"))

    def x_pass(d):
        slot = xg.at[ext_behind(d) * 2 + core, lead_rows]
        move(slot, slot, sem("s_x"), sem("x_pass"), row=core_mate).start()

    repeat(ext_steps, x_pass)
    with scope("x_rest"):
        arrived(xg.at[0], sem("x_mate"))
        arrived(xg.at[pl.ds(0, 2 * (exts - 1)), rest_rows], sem("x_rest"))
    with scope("x_pass"):
        arrived(xg.at[pl.ds(0, exts - 1), lead_rows], sem("x_pass"))

    depth = rows * nodes

    def product(p, y, g):
        left = tile[p, y, pl.ds(g * group, group)].reshape(group * sub, depth)
        panel = xg[...].reshape(depth, width)
        return jnp.dot(left, panel, preferred_element_type=F32).reshape(group, sub, width)

    def for_mate(p):
        def one(g):
            mate_part[p, pl.ds(g * group, group)] = product(p, 1 - low, g).astype(BF16)

        repeat_all(groups, one)

        def send(d):
            z = high_ahead(d)
            move(
                mate_part.at[p, z], mate_in.at[p, z], sem("s_ry"), sem("ry", p * half + d), col=mate
            ).start()

        repeat(others, send)
        send(0)

    def for_me(p):
        def one(g):
            own[p, pl.ds(g * group, group)] = product(p, low, g)

        repeat_all(groups, one)

    def repeat_all(count, step):
        if count == 1:
            step(0)
        else:

            def one(g, unused):
                step(g)
                return unused

            lax.fori_loop(0, count, one, 0)

    with scope("fwd"):
        for p in range(PARTS):
            for_mate(p)
        for p in range(PARTS):
            for_me(p)

    def turn(p, y):
        def one(g):
            for k in range(col_blocks):
                left = tile[p, y, pl.ds(g * group, group), :, pl.ds(k * block, block)]
                tile_t[p, y, g, pl.ds(k * block, block), :] = left.reshape(group * sub, block).T

        repeat_all(groups, one)

    with scope("turn"):
        for p in range(PARTS):
            for y in range(2):
                turn(p, y)

    def to_high(p):
        def one(d):
            z = high_ahead(d)
            arrived(mate_in.at[p, z], sem("ry", p * half + d))
            part[p, z] = (own[p, z] + mate_in[p, z].astype(F32)).astype(BF16)
            move(
                part.at[p, z], part_in.at[p, high], sem("s_rz"), sem("rz", p), col=z * 2 + low
            ).start()

        repeat(others, one)
        arrived(mate_in.at[p, high], sem("ry", p * half))
        keep[p] = own[p, high] + mate_in[p, high].astype(F32)

    for p in range(PARTS):
        with scope("to_high%d" % p):
            to_high(p)

    load_w.wait()
    load_og.wait()
    scale = 1.0 / math.sqrt(nodes * rows * cols)
    piece = width // plane
    over_nodes = (((0,), (0,)), ((), ()))
    both = pl.ds(0, FEATS)

    def spread(f, p, index):
        mine = up.at[f, p, low, high]
        repeat(
            others,
            lambda d: move(
                mine, mine, sem("s_gz"), sem("gz", index * (half - 1) + d - 1),
                col=high_ahead(d) * 2 + low,
            ).start(),
        )
        move(mine, mine, sem("s_gy"), sem("gy", index), col=mate).start()

    def middle(p):
        with scope("rz%d" % p):
            arrived(part_in.at[p, pl.ds(0, half - 1)], sem("rz", p))

        def add(d):
            keep[p] += part_in[p, high_behind(d)].astype(F32)

        repeat(others, add)
        mixed = keep[p]
        pre = split_dot(mixed, w_ref[...], (((1,), (0,)), ((), ())))
        decay = jnp.exp(jnp.minimum(pre, 0.0))
        slope = jnp.where(pre > 0, 1.0, decay)
        some = pl.ds(p * sub, sub)
        upstream = (og_ref[some].astype(F32) * slope).astype(BF16)
        for f in range(FEATS):
            up[f, p, low, high] = upstream[:, f * fw : (f + 1) * fw]
        if p < PARTS - 1:
            spread(both, p, 0)
        else:
            for f in range(FEATS):
                spread(f, p, 1 + f)
        out_ref[some] = jnp.where(pre > 0, pre, decay - 1.0).astype(BF16)
        share = split_dot(mixed, upstream, over_nodes)
        if p == 0:
            term_sum[...] = share
        else:
            share = term_sum[...] + share
            term[...] = (share * scale).reshape(plane, piece, width).astype(BF16)

    for p in range(PARTS):
        with scope("middle%d" % p):
            middle(p)

    def to_spots(src, dst, sent, got):
        def one(d):
            spot = spot_ahead(d)
            move(
                src(spot), dst.at[my_spot], sent, got,
                row=spot // 2, col=high * 2 + lax.rem(spot, 2),
            ).start()

        repeat(list(range(1, plane)), one)

    with scope("w1_send"):
        to_spots(lambda spot: term.at[spot], w1_in, sem("s_w", 0), sem("w", 0))
        w1_in[my_spot] = term[my_spot]

    def region(f, p, z):
        return up.at[f, p, low, z]

    def pass_on(f, p, index):
        def one(d):
            slot = region(f, p, high_behind(d))
            arrived(slot, sem("gz", index * (half - 1) + d - 1))
            move(slot, slot, sem("s_gy"), sem("gy", index), col=mate).start()

        repeat(others, one)

    def back(f, p, y, first=False):
        def one(g):
            right = up[f, p, y, pl.ds(g * group, group)].reshape(group * sub, fw)
            got = jnp.dot(tile_t[p, y, g], right, preferred_element_type=F32)
            if first:
                acc[f] = got
            else:
                acc[f] += got

        if first and groups > 1:
            acc[f] = jnp.zeros(acc.shape[1:], F32)
            first = False
        repeat_all(groups, one)

    with scope("gz_p0"):
        pass_on(both, 0, 0)
    for f in range(FEATS):
        back(f, 0, low, first=True)
    for f in range(FEATS):
        with scope("gz_p1_%d" % f):
            pass_on(f, 1, 1 + f)
    with scope("w1_wait"):
        arrived(w1_in.at[pl.ds(0, plane - 1)], sem("w", 0))
        w2_in[high] = jnp.sum(w1_in[...].astype(F32), axis=0).astype(BF16)
        repeat(
            others,
            lambda d: move(
                w2_in.at[high], w2_in.at[high], sem("s_w", 1), sem("w", 1),
                col=high_ahead(d) * 2 + low,
            ).start(),
        )
    for f in range(FEATS):
        back(f, 1, low)

    with scope("gy_p0"):
        arrived(up.at[both, 0, 1 - low], sem("gy", 0))
    for f in range(FEATS):
        back(f, 0, 1 - low)

    def block_of(r):
        return pl.ds(pl.multiple_of(r * nodes, nodes), nodes)

    def lead_of(r):
        return pl.ds(pl.multiple_of(r * nodes, nodes), lead)

    def rest_of(r):
        return pl.ds(pl.multiple_of(r * nodes + lead, rest), rest)

    def launch(f):
        pc[f, core_mate] = acc[f, block_of(core_mate)].astype(BF16)

        def pre(d):
            far = ext_ahead(d)
            other = far * 2 + 1 - core
            pc[f, other] = acc[f, block_of(other)].astype(BF16)
            move(
                pc.at[f, other, lead_rows], pre_in.at[f, far], sem("s_c"), sem("c_pre", f),
                row=core_mate,
            ).start()

        repeat(ext_steps, pre)

        def direct(d):
            far = ext_ahead(d)
            same = far * 2 + core
            other = far * 2 + 1 - core
            move(
                pc.at[f, other, rest_rows], rest_in.at[f, my_row], sem("s_c"), sem("c_rest", f),
                row=other,
            ).start()
            pc[f, same, rest_rows] = acc[f, rest_of(same)].astype(BF16)
            move(
                pc.at[f, same, rest_rows], rest_in.at[f, my_row], sem("s_c"), sem("c_rest", f),
                row=same,
            ).start()

        repeat(ext_steps, direct)
        move(pc.at[f, core_mate], pc_mate.at[f], sem("s_c"), sem("c_mate", f), row=core_mate).start()

    def relay(f):
        arrived(pre_in.at[f, pl.ds(0, exts - 1)], sem("c_pre", f))

        def one(d):
            far = ext_ahead(d)
            same = far * 2 + core
            pc[f, same, lead_rows] = (
                acc[f, lead_of(same)] + pre_in[f, far].astype(F32)
            ).astype(BF16)
            move(
                pc.at[f, same, lead_rows], lead_in.at[f, ext], sem("s_c"), sem("c_lead", f),
                row=same,
            ).start()

        repeat(ext_steps, one)

    def gather_grad(f):
        arrived(pc_mate.at[f], sem("c_mate", f))
        acc[f, block_of(my_row)] += pc_mate[f].astype(F32)
        arrived(rest_in.at[f, pl.ds(0, 2 * (exts - 1))], sem("c_rest", f))

        def add_rest(d):
            for k in range(2):
                acc[f, rest_of(my_row)] += rest_in[f, ext_behind(d) * 2 + k].astype(F32)

        repeat(ext_steps, add_rest)
        arrived(lead_in.at[f, pl.ds(0, exts - 1)], sem("c_lead", f))

        def add_lead(d):
            acc[f, lead_of(my_row)] += lead_in[f, ext_behind(d)].astype(F32)

        repeat(ext_steps, add_lead)
        some = pl.ds(f * fw, fw)
        return split_dot(acc[f, block_of(my_row)], w_ref[:, some], (((1,), (1,)), ((), ())))

    for f in range(FEATS):
        with scope("gy_p1_%d" % f):
            arrived(up.at[f, 1, 1 - low], sem("gy", 1 + f))
        back(f, 1, 1 - low)
        with scope("launch%d" % f):
            launch(f)
        if f < FEATS - 1:
            with scope("relay%d" % f):
                relay(f)
    with scope("w2_wait"):
        arrived(w2_in.at[pl.ds(0, half - 1)], sem("w", 1))
        w3_in[my_spot] = jnp.sum(w2_in[...].astype(F32), axis=0).astype(BF16)
        to_spots(lambda spot: w3_in.at[my_spot], w3_in, sem("s_w", 2), sem("w", 2))
    with scope("relay_last"):
        relay(FEATS - 1)
    grad = 0.0
    for f in range(FEATS):
        with scope("grad%d" % f):
            grad = grad + gather_grad(f)
    ig_ref[...] = grad.astype(BF16)

    with scope("gone"):
        gone(xg.at[pl.ds(0, rows - 1)], sem("s_x"))
        gone(mate_part, sem("s_ry"))
        gone(part.at[:, pl.ds(0, half - 1)], sem("s_rz"))
        gone(up.at[:, :, low, pl.ds(0, half - 1)], sem("s_gz"))
        gone(up.at[:, :, low], sem("s_gy"))
        gone(pc.at[:, pl.ds(0, rows - 1)], sem("s_c"))
        gone(term.at[pl.ds(0, plane - 1)], sem("s_w", 0))
        gone(w2_in.at[pl.ds(0, half - 1)], sem("s_w", 1))
        gone(w3_in.at[pl.ds(0, plane - 1)], sem("s_w", 2))
    with scope("w3_wait"):
        arrived(w3_in.at[pl.ds(0, plane - 1)], sem("w", 2))
    wg_ref[...] = w3_in[...].reshape(width, width).astype(F32)


def finish(out_ref, ig_ref, wg_ref, out_hbm, ig_hbm, wg_hbm, sem):
    trio = ((out_ref, out_hbm), (ig_ref, ig_hbm), (wg_ref, wg_hbm))
    copies = [pltpu.make_async_copy(a, b, sem.at[i]) for i, (a, b) in enumerate(trio)]
    for copy in copies:
        copy.start()
    for copy in copies:
        copy.wait()


def body(node_features, layer_weight, output_grad, block_values, block_position, tile_count):
    rows, cols = lax.axis_size("row"), lax.axis_size("col")
    nodes, width = node_features.shape
    slots, block = block_values.shape[2], block_values.shape[3]
    half, exts, plane = cols // 2, rows // 2, 2 * rows
    assert nodes == block and cols == 2 * half and rows == 2 * exts
    sub, fw = nodes // PARTS, width // FEATS
    lead = nodes // 2
    rest = nodes - lead
    group = min(half, 4)
    groups = half // group
    piece = width // plane
    depth = rows * nodes
    place = pl.BlockSpec(memory_space=pl.ANY)
    pinned = pl.BlockSpec(memory_space=pltpu.HBM)
    inside = pl.BlockSpec(memory_space=pltpu.VMEM)
    dma = pltpu.SemaphoreType.DMA
    vmem = pltpu.VMEM
    shapes = (
        jax.ShapeDtypeStruct((nodes, width), BF16),
        jax.ShapeDtypeStruct((nodes, width), BF16),
        jax.ShapeDtypeStruct((width, width), F32),
    )
    results = pl.pallas_call(
        functools.partial(kernel, rows, cols),
        out_shape=(
            vmem((nodes, width), BF16),
            vmem((nodes, width), BF16),
            vmem((width, width), F32),
        ),
        in_specs=[pinned, pinned, place, place, place, place],
        out_specs=(inside, inside, inside),
        scratch_shapes=[
            pltpu.SMEM((slots,), jnp.int32),
            pltpu.SMEM((1, 1), jnp.int32),
            vmem((slots + 1, block, block), BF16),
            vmem((width, width), BF16),
            vmem((nodes, width), BF16),
            vmem((rows, nodes, width), BF16),
            vmem((PARTS, 2, half, sub, depth), BF16),
            vmem((PARTS, 2, groups, depth, group * sub), BF16),
            vmem((PARTS, half, sub, width), BF16),
            vmem((PARTS, half, sub, width), BF16),
            vmem((PARTS, half, sub, width), F32),
            vmem((PARTS, half, sub, width), BF16),
            vmem((PARTS, half, sub, width), BF16),
            vmem((PARTS, sub, width), F32),
            vmem((FEATS, PARTS, 2, half, sub, fw), BF16),
            vmem((FEATS, depth, fw), F32),
            vmem((width, width), F32),
            vmem((plane, piece, width), BF16),
            vmem((plane, piece, width), BF16),
            vmem((half, piece, width), BF16),
            vmem((plane, piece, width), BF16),
            vmem((FEATS, rows, nodes, fw), BF16),
            vmem((FEATS, nodes, fw), BF16),
            vmem((FEATS, exts, lead, fw), BF16),
            vmem((FEATS, rows, rest, fw), BF16),
            vmem((FEATS, exts, lead, fw), BF16),
            dma((sum(counts(rows, cols).values()),)),
        ],
        compiler_params=pltpu.CompilerParams(collective_id=0, has_side_effects=True),
    )(
        block_position.reshape(slots),
        tile_count,
        node_features,
        layer_weight,
        output_grad,
        block_values.reshape(slots, block, block),
    )
    return pl.pallas_call(
        finish,
        out_shape=shapes,
        in_specs=[inside] * 3,
        out_specs=(place,) * 3,
        scratch_shapes=[
            dma((3,)),
        ],
        compiler_params=pltpu.CompilerParams(vmem_limit_bytes=4 << 20),
    )(*results)


def solution(mesh):
    in_specs = (
        P(("row", "col"), None),
        P(),
        P(("row", "col"), None),
        P("row", "col", None, None, None),
        P("row", "col", None),
        P("row", "col"),
    )
    out_specs = (P(("row", "col"), None), P(("row", "col"), None), P())
    return jax.shard_map(body, mesh=mesh, in_specs=in_specs, out_specs=out_specs, check_vma=False)
```

time: 40.2 us -> 37.5 us (0.933)
  Pallas kernels: 38.7 us -> 36.1 us
    pallas_call x1, Pallas kernels: 38 us -> 35.3 us  [body(): pl.pallas_call(functools.partial(kernel, rows, cols), out_shape=(vmem((no...]
where the time goes in v1:
time: 37.5 us; the launch traced here: 37.4 us
  Pallas kernels  36.1 us (96%)
  between operations  1.29 us (3%)
    pallas_call x1, Pallas kernels, body(): pl.pallas_call(functools.partial(kernel, rows, cols), out_shape=(vmem((no...  35.3 us
    pallas_call x1, Pallas kernels, body(): pl.pallas_call(finish, out_shape=shapes, in_specs=[inside] * 3, out_specs...  0.77 us

profile of v1, /device:TPU:0, one launch (start us, length us, event | category | flops | bytes accessed | tf_op | source)
XLA Modules:
  0.0 37.4 jit_solution(8046539465329175527)
XLA Ops:
  1.3 35.3 %shard_map.85 = (bf16[128,256]{1,0:T(8,128)(2,1)S(1)}, bf16[128,256]{1,0:T(8,128)(2,1)S(1)}, f32[256,256]{1,0:T(8,128)S(1)}) custom-call(s32[24]{0:T(128)} %bitcast.3, s32[1,1]{1,0:T(1,128)S(6)} %copy.9.count_hbm, bf16[128,256]{1,0:T(8,128)(2,1)} %x_hbm.1, bf16[256,256]{1,0:T(8,128)(2,1)} %w_hbm.1, bf16[128,256]{1,0:T(8,128)(2,1)} %og_hbm.1, ...), custom_call_target="tpu_custom_call" | custom-call | tf_op jit(solution)/shard_map/pallas_call | solution.py:592
  36.6 0.8 %shard_map.86 = (bf16[128,256]{1,0:T(8,128)(2,1)}, bf16[128,256]{1,0:T(8,128)(2,1)}, f32[256,256]{1,0:T(8,128)}) custom-call(bf16[128,256]{1,0:T(8,128)(2,1)S(1)} %get-tuple-element.6.out_ref, bf16[128,256]{1,0:T(8,128)(2,1)S(1)} %get-tuple-element.7.ig_ref, f32[256,256]{1,0:T(8,128)S(1)} %get-tuple-element.8.wg_ref), custom_call_target="tpu_custom_call" | custom-call | tf_op jit(solution)/shard_map/pallas_call | solution.py:639

commit v2 on v1

--- a/solution.py
+++ b/solution.py
@@ -38,19 +38,17 @@
 def counts(rows, cols):
     half = cols // 2
     return {
-        "load": 6,
-        "x_mate": 1,
-        "x_lead": 1,
-        "x_rest": 1,
-        "x_pass": 1,
-        "ry": PARTS * half,
+        "load": 5 + FEATS,
+        "x_mate": FEATS,
+        "x_lead": FEATS,
+        "x_rest": FEATS,
+        "x_pass": FEATS,
+        "yc": PARTS * FEATS * (half // 2),
+        "yb": PARTS * (half // 2),
         "rz": PARTS,
         "gz": (1 + FEATS) * (half - 1),
         "gy": 1 + FEATS,
-        "c_mate": FEATS,
-        "c_pre": FEATS,
-        "c_rest": FEATS,
-        "c_lead": FEATS,
+        "c": FEATS,
         "w": 3,
         "s_x": 1,
         "s_ry": 1,
@@ -96,10 +94,7 @@
     w2_in,
     w3_in,
     pc,
-    pc_mate,
-    pre_in,
-    rest_in,
-    lead_in,
+    pc_in,
     sems,
 ):
     scope = jax.named_scope
@@ -124,7 +119,9 @@
     rest = nodes - lead
     group = min(half, 4)
     groups = half // group
-    others = [half // 2] + [d for d in range(1, half) if d != half // 2]
+    wing = half // 2
+    side = high // wing
+    rank = lax.rem(high, wing)
     ext_steps = list(range(1, exts))
     lead_rows, rest_rows = pl.ds(0, lead), pl.ds(lead, rest)
 
@@ -136,11 +133,28 @@
     def sem(name, index=0):
         return sems.at[base[name] + index]
 
-    def high_ahead(d):
-        return lax.rem(high + d, half)
-
-    def high_behind(d):
-        return lax.rem(high + half - d, half)
+    def across(step):
+        def one(j):
+            far = (1 - side) * wing + lax.rem(wing - 1 - rank + j, wing)
+            step(j, far, far)
+
+        repeat(list(range(wing)), one)
+
+    def beside(step):
+        def one(j):
+            to = side * wing + lax.rem(rank + j, wing)
+            come = side * wing + lax.rem(rank + wing - j, wing)
+            step(wing - 1 + j, to, come)
+
+        repeat(list(range(1, wing)), one)
+
+    def far_first(step):
+        across(step)
+        beside(step)
+
+    def near_first(step):
+        beside(step)
+        across(step)
 
     def ext_ahead(d):
         return lax.rem(ext + d, exts)
@@ -168,12 +182,17 @@
         move(ref, ref, sent, sem("x_mate"), col=mate).wait_send()
 
     load = pltpu.make_async_copy(values_hbm, values.at[pl.ds(0, slots)], sem("load", 0))
-    load_x = pltpu.make_async_copy(x_hbm, xg.at[my_row], sem("load", 1))
+    load_x = [
+        pltpu.make_async_copy(
+            x_hbm.at[:, pl.ds(f * fw, fw)], xg.at[f, my_row], sem("load", 5 + f)
+        )
+        for f in range(FEATS)
+    ]
     load_w = pltpu.make_async_copy(w_hbm, w_ref, sem("load", 2))
     load_og = pltpu.make_async_copy(og_hbm, og_ref, sem("load", 3))
     load_position = pltpu.make_async_copy(position_hbm, position, sem("load", 4))
-    load_count = pltpu.make_async_copy(count_hbm, count, sem("load", 5))
-    for one in (load_x, load_position, load_count, load, load_w, load_og):
+    load_count = pltpu.make_async_copy(count_hbm, count, sem("load", 1))
+    for one in (*load_x, load_position, load_count, load, load_w, load_og):
         one.start()
 
     barrier = pltpu.get_barrier_semaphore()
@@ -181,7 +200,7 @@
     def greet(**target):
         pl.semaphore_signal(barrier, inc=1, device_id=target, device_id_type=MESH)
 
-    repeat(others, lambda d: greet(col=high_ahead(d) * 2 + low))
+    far_first(lambda t, to, come: greet(col=to * 2 + low))
 
     def greet_spot(d):
         spot = spot_ahead(d)
@@ -189,28 +208,32 @@
 
     repeat(list(range(1, plane)), greet_spot)
     values[slots] = jnp.zeros((block, block), BF16)
-    load_x.wait()
+    for one in load_x:
+        one.wait()
     with scope("bar"):
         pl.semaphore_wait(barrier, plane - 1 + half - 1)
 
-    mine = xg.at[my_row]
-
-    def x_lead(d):
-        move(
-            mine.at[lead_rows], xg.at[my_row, lead_rows], sem("s_x"), sem("x_lead"),
-            row=ext_ahead(d) * 2 + core,
-        ).start()
-
-    def x_rest(d):
-        for to in (core, 1 - core):
+    def x_send(f):
+        mine = xg.at[f, my_row]
+
+        def send_lead(d):
             move(
-                mine.at[rest_rows], xg.at[my_row, rest_rows], sem("s_x"), sem("x_rest"),
-                row=ext_ahead(d) * 2 + to,
-            ).start()
-
-    repeat(ext_steps, x_lead)
-    move(mine, mine, sem("s_x"), sem("x_mate"), row=core_mate).start()
-    repeat(ext_steps, x_rest)
+                mine.at[lead_rows], mine.at[lead_rows], sem("s_x"), sem("x_lead", f),
+                row=ext_ahead(d) * 2 + core,
+            ).start()
+
+        def send_rest(d):
+            for to in (core, 1 - core):
+                move(
+                    mine.at[rest_rows], mine.at[rest_rows], sem("s_x"), sem("x_rest", f),
+                    row=ext_ahead(d) * 2 + to,
+                ).start()
+
+        repeat(ext_steps, send_lead)
+        move(mine, mine, sem("s_x"), sem("x_mate", f), row=core_mate).start()
+        repeat(ext_steps, send_rest)
+
+    x_send(0)
 
     with scope("load"):
         load_position.wait()
@@ -242,47 +265,27 @@
 
             lax.fori_loop(0, half, build_pair, jnp.int32(0))
 
-    with scope("x_lead"):
-        arrived(xg.at[pl.ds(0, exts - 1), lead_rows], sem("x_lead"))
-
-    def x_pass(d):
-        slot = xg.at[ext_behind(d) * 2 + core, lead_rows]
-        move(slot, slot, sem("s_x"), sem("x_pass"), row=core_mate).start()
-
-    repeat(ext_steps, x_pass)
-    with scope("x_rest"):
-        arrived(xg.at[0], sem("x_mate"))
-        arrived(xg.at[pl.ds(0, 2 * (exts - 1)), rest_rows], sem("x_rest"))
-    with scope("x_pass"):
-        arrived(xg.at[pl.ds(0, exts - 1), lead_rows], sem("x_pass"))
+    for f in range(1, FEATS):
+        x_send(f)
 
     depth = rows * nodes
 
-    def product(p, y, g):
-        left = tile[p, y, pl.ds(g * group, group)].reshape(group * sub, depth)
-        panel = xg[...].reshape(depth, width)
-        return jnp.dot(left, panel, preferred_element_type=F32).reshape(group, sub, width)
-
-    def for_mate(p):
-        def one(g):
-            mate_part[p, pl.ds(g * group, group)] = product(p, 1 - low, g).astype(BF16)
-
-        repeat_all(groups, one)
-
-        def send(d):
-            z = high_ahead(d)
-            move(
-                mate_part.at[p, z], mate_in.at[p, z], sem("s_ry"), sem("ry", p * half + d), col=mate
-            ).start()
-
-        repeat(others, send)
-        send(0)
-
-    def for_me(p):
-        def one(g):
-            own[p, pl.ds(g * group, group)] = product(p, low, g)
-
-        repeat_all(groups, one)
+    def x_relay(f):
+        with scope("x_lead%d" % f):
+            arrived(xg.at[f, pl.ds(0, exts - 1), lead_rows], sem("x_lead", f))
+
+        def one(d):
+            slot = xg.at[f, ext_behind(d) * 2 + core, lead_rows]
+            move(slot, slot, sem("s_x"), sem("x_pass", f), row=core_mate).start()
+
+        repeat(ext_steps, one)
+
+    def x_wait(f):
+        with scope("x_rest%d" % f):
+            arrived(xg.at[f, 0], sem("x_mate", f))
+            arrived(xg.at[f, pl.ds(0, 2 * (exts - 1)), rest_rows], sem("x_rest", f))
+        with scope("x_pass%d" % f):
+            arrived(xg.at[f, pl.ds(0, exts - 1), lead_rows], sem("x_pass", f))
 
     def repeat_all(count, step):
         if count == 1:
@@ -295,11 +298,63 @@
 
             lax.fori_loop(0, count, one, 0)
 
-    with scope("fwd"):
+    def product(p, f, y, g):
+        left = tile[p, y, pl.ds(g * group, group)].reshape(group * sub, depth)
+        panel = xg[f].reshape(depth, fw)
+        return jnp.dot(left, panel, preferred_element_type=F32).reshape(group, sub, fw)
+
+    def yc(p, f, j):
+        return sem("yc", (p * FEATS + f) * wing + j)
+
+    def yb(p, j):
+        return sem("yb", p * wing + j)
+
+    def for_mate(p, f):
+        def one(g):
+            mate_part[p, f, pl.ds(g * group, group)] = product(p, f, 1 - low, g).astype(BF16)
+
+        repeat_all(groups, one)
+
+        def send(j, z, unused):
+            move(
+                mate_part.at[p, f, z], mate_in.at[p, f, z], sem("s_ry"), yc(p, f, j), col=mate
+            ).start()
+
+        across(send)
+
+    def for_mate_near(p):
+        def send(t, z, unused):
+            move(
+                mate_part.at[p, :, z], mate_in.at[p, :, z], sem("s_ry"), yb(p, t - wing), col=mate
+            ).start()
+
+        beside(send)
+        send(2 * wing - 1, high, high)
+
+    def for_me(p, f):
+        def one(g):
+            own[p, f, pl.ds(g * group, group)] = product(p, f, low, g)
+
+        repeat_all(groups, one)
+
+    x_relay(0)
+    x_wait(0)
+    with scope("fwd0"):
+        for_mate(0, 0)
+    for f in range(1, FEATS):
+        x_relay(f)
+    for f in range(1, FEATS):
+        x_wait(f)
+        for_mate(0, f)
+    with scope("fwd1"):
+        for p in range(1, PARTS):
+            for f in range(FEATS):
+                for_mate(p, f)
         for p in range(PARTS):
-            for_mate(p)
+            for_mate_near(p)
         for p in range(PARTS):
-            for_me(p)
+            for f in range(FEATS):
+                for_me(p, f)
 
     def turn(p, y):
         def one(g):
@@ -314,22 +369,37 @@
             for y in range(2):
                 turn(p, y)
 
-    def to_high(p):
-        def one(d):
-            z = high_ahead(d)
-            arrived(mate_in.at[p, z], sem("ry", p * half + d))
-            part[p, z] = (own[p, z] + mate_in[p, z].astype(F32)).astype(BF16)
+    def to_across(p, f):
+        def one(j, z, unused):
+            arrived(mate_in.at[p, f, z], yc(p, f, j))
+            part[p, f, z] = (own[p, f, z] + mate_in[p, f, z].astype(F32)).astype(BF16)
             move(
-                part.at[p, z], part_in.at[p, high], sem("s_rz"), sem("rz", p), col=z * 2 + low
-            ).start()
-
-        repeat(others, one)
-        arrived(mate_in.at[p, high], sem("ry", p * half))
-        keep[p] = own[p, high] + mate_in[p, high].astype(F32)
+                part.at[p, f, z], part_in.at[p, f, high], sem("s_rz"), sem("rz", p),
+                col=z * 2 + low,
+            ).start()
+
+        across(one)
+
+    def to_beside(p):
+        def one(t, z, unused):
+            arrived(mate_in.at[p, :, z], yb(p, t - wing))
+            part[p, :, z] = (own[p, :, z] + mate_in[p, :, z].astype(F32)).astype(BF16)
+            move(
+                part.at[p, :, z], part_in.at[p, :, high], sem("s_rz"), sem("rz", p),
+                col=z * 2 + low,
+            ).start()
+
+        beside(one)
+        arrived(mate_in.at[p, :, high], yb(p, wing - 1))
+        keep[p] = own[p, :, high] + mate_in[p, :, high].astype(F32)
 
     for p in range(PARTS):
-        with scope("to_high%d" % p):
-            to_high(p)
+        for f in range(FEATS):
+            with scope("across%d%d" % (p, f)):
+                to_across(p, f)
+    for p in range(PARTS):
+        with scope("beside%d" % p):
+            to_beside(p)
 
     load_w.wait()
     load_og.wait()
@@ -340,24 +410,22 @@
 
     def spread(f, p, index):
         mine = up.at[f, p, low, high]
-        repeat(
-            others,
-            lambda d: move(
-                mine, mine, sem("s_gz"), sem("gz", index * (half - 1) + d - 1),
-                col=high_ahead(d) * 2 + low,
-            ).start(),
+        far_first(
+            lambda t, z, unused: move(
+                mine, mine, sem("s_gz"), sem("gz", index * (half - 1) + t), col=z * 2 + low
+            ).start()
         )
         move(mine, mine, sem("s_gy"), sem("gy", index), col=mate).start()
 
     def middle(p):
         with scope("rz%d" % p):
-            arrived(part_in.at[p, pl.ds(0, half - 1)], sem("rz", p))
-
-        def add(d):
-            keep[p] += part_in[p, high_behind(d)].astype(F32)
-
-        repeat(others, add)
-        mixed = keep[p]
+            arrived(part_in.at[p, :, pl.ds(0, half - 1)], sem("rz", p))
+
+        def add(t, unused, z):
+            keep[p] += part_in[p, :, z].astype(F32)
+
+        near_first(add)
+        mixed = jnp.concatenate([keep[p, f] for f in range(FEATS)], axis=1)
         pre = split_dot(mixed, w_ref[...], (((1,), (0,)), ((), ())))
         decay = jnp.exp(jnp.minimum(pre, 0.0))
         slope = jnp.where(pre > 0, 1.0, decay)
@@ -400,12 +468,12 @@
         return up.at[f, p, low, z]
 
     def pass_on(f, p, index):
-        def one(d):
-            slot = region(f, p, high_behind(d))
-            arrived(slot, sem("gz", index * (half - 1) + d - 1))
+        def one(t, unused, z):
+            slot = region(f, p, z)
+            arrived(slot, sem("gz", index * (half - 1) + t))
             move(slot, slot, sem("s_gy"), sem("gy", index), col=mate).start()
 
-        repeat(others, one)
+        near_first(one)
 
     def back(f, p, y, first=False):
         def one(g):
@@ -431,12 +499,10 @@
     with scope("w1_wait"):
         arrived(w1_in.at[pl.ds(0, plane - 1)], sem("w", 0))
         w2_in[high] = jnp.sum(w1_in[...].astype(F32), axis=0).astype(BF16)
-        repeat(
-            others,
-            lambda d: move(
-                w2_in.at[high], w2_in.at[high], sem("s_w", 1), sem("w", 1),
-                col=high_ahead(d) * 2 + low,
-            ).start(),
+        far_first(
+            lambda t, z, unused: move(
+                w2_in.at[high], w2_in.at[high], sem("s_w", 1), sem("w", 1), col=z * 2 + low
+            ).start()
         )
     for f in range(FEATS):
         back(f, 1, low)
@@ -449,75 +515,30 @@
     def block_of(r):
         return pl.ds(pl.multiple_of(r * nodes, nodes), nodes)
 
-    def lead_of(r):
-        return pl.ds(pl.multiple_of(r * nodes, nodes), lead)
-
-    def rest_of(r):
-        return pl.ds(pl.multiple_of(r * nodes + lead, rest), rest)
-
     def launch(f):
-        pc[f, core_mate] = acc[f, block_of(core_mate)].astype(BF16)
-
-        def pre(d):
-            far = ext_ahead(d)
-            other = far * 2 + 1 - core
-            pc[f, other] = acc[f, block_of(other)].astype(BF16)
-            move(
-                pc.at[f, other, lead_rows], pre_in.at[f, far], sem("s_c"), sem("c_pre", f),
-                row=core_mate,
-            ).start()
-
-        repeat(ext_steps, pre)
-
-        def direct(d):
-            far = ext_ahead(d)
-            same = far * 2 + core
-            other = far * 2 + 1 - core
-            move(
-                pc.at[f, other, rest_rows], rest_in.at[f, my_row], sem("s_c"), sem("c_rest", f),
-                row=other,
-            ).start()
-            pc[f, same, rest_rows] = acc[f, rest_of(same)].astype(BF16)
-            move(
-                pc.at[f, same, rest_rows], rest_in.at[f, my_row], sem("s_c"), sem("c_rest", f),
-                row=same,
-            ).start()
-
-        repeat(ext_steps, direct)
-        move(pc.at[f, core_mate], pc_mate.at[f], sem("s_c"), sem("c_mate", f), row=core_mate).start()
-
-    def relay(f):
-        arrived(pre_in.at[f, pl.ds(0, exts - 1)], sem("c_pre", f))
-
-        def one(d):
-            far = ext_ahead(d)
-            same = far * 2 + core
-            pc[f, same, lead_rows] = (
-                acc[f, lead_of(same)] + pre_in[f, far].astype(F32)
-            ).astype(BF16)
-            move(
-                pc.at[f, same, lead_rows], lead_in.at[f, ext], sem("s_c"), sem("c_lead", f),
-                row=same,
-            ).start()
-
-        repeat(ext_steps, one)
+        def one(r):
+            pc[f, r] = acc[f, block_of(r)].astype(BF16)
+            move(pc.at[f, r], pc_in.at[f, my_row], sem("s_c"), sem("c", f), row=r).start()
+
+        def outside(d):
+            one(ext_ahead(d) * 2 + core)
+            one(ext_ahead(d) * 2 + 1 - core)
+
+        repeat(ext_steps, outside)
+        one(core_mate)
 
     def gather_grad(f):
-        arrived(pc_mate.at[f], sem("c_mate", f))
-        acc[f, block_of(my_row)] += pc_mate[f].astype(F32)
-        arrived(rest_in.at[f, pl.ds(0, 2 * (exts - 1))], sem("c_rest", f))
-
-        def add_rest(d):
+        arrived(pc_in.at[f, pl.ds(0, rows - 1)], sem("c", f))
+
+        def add(r):
+            acc[f, block_of(my_row)] += pc_in[f, r].astype(F32)
+
+        def outside(d):
             for k in range(2):
-                acc[f, rest_of(my_row)] += rest_in[f, ext_behind(d) * 2 + k].astype(F32)
-
-        repeat(ext_steps, add_rest)
-        arrived(lead_in.at[f, pl.ds(0, exts - 1)], sem("c_lead", f))
-
-        def add_lead(d):
-            acc[f, lead_of(my_row)] += lead_in[f, ext_behind(d)].astype(F32)
-
-        repeat(ext_steps, add_lead)
+                add(ext_behind(d) * 2 + k)
+
+        repeat(ext_steps, outside)
+        add(core_mate)
         some = pl.ds(f * fw, fw)
         return split_dot(acc[f, block_of(my_row)], w_ref[:, some], (((1,), (1,)), ((), ())))
 
@@ -527,15 +548,10 @@
         back(f, 1, 1 - low)
         with scope("launch%d" % f):
             launch(f)
-        if f < FEATS - 1:
-            with scope("relay%d" % f):
-                relay(f)
     with scope("w2_wait"):
         arrived(w2_in.at[pl.ds(0, half - 1)], sem("w", 1))
         w3_in[my_spot] = jnp.sum(w2_in[...].astype(F32), axis=0).astype(BF16)
         to_spots(lambda spot: w3_in.at[my_spot], w3_in, sem("s_w", 2), sem("w", 2))
-    with scope("relay_last"):
-        relay(FEATS - 1)
     grad = 0.0
     for f in range(FEATS):
         with scope("grad%d" % f):
@@ -543,9 +559,9 @@
     ig_ref[...] = grad.astype(BF16)
 
     with scope("gone"):
-        gone(xg.at[pl.ds(0, rows - 1)], sem("s_x"))
+        gone(xg.at[:, pl.ds(0, rows - 1)], sem("s_x"))
         gone(mate_part, sem("s_ry"))
-        gone(part.at[:, pl.ds(0, half - 1)], sem("s_rz"))
+        gone(part.at[:, :, pl.ds(0, half - 1)], sem("s_rz"))
         gone(up.at[:, :, low, pl.ds(0, half - 1)], sem("s_gz"))
         gone(up.at[:, :, low], sem("s_gy"))
         gone(pc.at[:, pl.ds(0, rows - 1)], sem("s_c"))
@@ -604,15 +620,15 @@
             vmem((slots + 1, block, block), BF16),
             vmem((width, width), BF16),
             vmem((nodes, width), BF16),
-            vmem((rows, nodes, width), BF16),
+            vmem((FEATS, rows, nodes, fw), BF16),
             vmem((PARTS, 2, half, sub, depth), BF16),
             vmem((PARTS, 2, groups, depth, group * sub), BF16),
-            vmem((PARTS, half, sub, width), BF16),
-            vmem((PARTS, half, sub, width), BF16),
-            vmem((PARTS, half, sub, width), F32),
-            vmem((PARTS, half, sub, width), BF16),
-            vmem((PARTS, half, sub, width), BF16),
-            vmem((PARTS, sub, width), F32),
+            vmem((PARTS, FEATS, half, sub, fw), BF16),
+            vmem((PARTS, FEATS, half, sub, fw), BF16),
+            vmem((PARTS, FEATS, half, sub, fw), F32),
+            vmem((PARTS, FEATS, half, sub, fw), BF16),
+            vmem((PARTS, FEATS, half, sub, fw), BF16),
+            vmem((PARTS, FEATS, sub, fw), F32),
             vmem((FEATS, PARTS, 2, half, sub, fw), BF16),
             vmem((FEATS, depth, fw), F32),
             vmem((width, width), F32),
@@ -621,10 +637,7 @@
             vmem((half, piece, width), BF16),
             vmem((plane, piece, width), BF16),
             vmem((FEATS, rows, nodes, fw), BF16),
-            vmem((FEATS, nodes, fw), BF16),
-            vmem((FEATS, exts, lead, fw), BF16),
-            vmem((FEATS, rows, rest, fw), BF16),
-            vmem((FEATS, exts, lead, fw), BF16),
+            vmem((FEATS, rows, nodes, fw), BF16),
             dma((sum(counts(rows, cols).values()),)),
         ],
         compiler_params=pltpu.CompilerParams(collective_id=0, has_side_effects=True),

time: 37.5 us -> 35.3 us (0.941)
  Pallas kernels: 36.1 us -> 33.9 us
    pallas_call x1, Pallas kernels: 35.3 us -> 33.1 us  [body(): pl.pallas_call(functools.partial(kernel, rows, cols), out_shape=(vmem((no...]
where the time goes in v2:
time: 35.3 us; the launch traced here: 35.1 us
  Pallas kernels  33.9 us (96%)
  between operations  1.29 us (4%)
    pallas_call x1, Pallas kernels, body(): pl.pallas_call(functools.partial(kernel, rows, cols), out_shape=(vmem((no...  33.1 us
    pallas_call x1, Pallas kernels, body(): pl.pallas_call(finish, out_shape=shapes, in_specs=[inside] * 3, out_specs...  0.77 us

profile of v2, /device:TPU:0, one launch (start us, length us, event | category | flops | bytes accessed | tf_op | source)
XLA Modules:
  0.0 35.1 jit_solution(87806615949468928)
XLA Ops:
  1.3 33.1 %shard_map.85 = (bf16[128,256]{1,0:T(8,128)(2,1)S(1)}, bf16[128,256]{1,0:T(8,128)(2,1)S(1)}, f32[256,256]{1,0:T(8,128)S(1)}) custom-call(s32[24]{0:T(128)} %bitcast.3, s32[1,1]{1,0:T(1,128)S(6)} %copy.9.count_hbm, bf16[128,256]{1,0:T(8,128)(2,1)} %x_hbm.1, bf16[256,256]{1,0:T(8,128)(2,1)} %w_hbm.1, bf16[128,256]{1,0:T(8,128)(2,1)} %og_hbm.1, ...), custom_call_target="tpu_custom_call" | custom-call | tf_op jit(solution)/shard_map/pallas_call | solution.py:608
  34.4 0.8 %shard_map.86 = (bf16[128,256]{1,0:T(8,128)(2,1)}, bf16[128,256]{1,0:T(8,128)(2,1)}, f32[256,256]{1,0:T(8,128)}) custom-call(bf16[128,256]{1,0:T(8,128)(2,1)S(1)} %get-tuple-element.6.out_ref, bf16[128,256]{1,0:T(8,128)(2,1)S(1)} %get-tuple-element.7.ig_ref, f32[256,256]{1,0:T(8,128)S(1)} %get-tuple-element.8.wg_ref), custom_call_target="tpu_custom_call" | custom-call | tf_op jit(solution)/shard_map/pallas_call | solution.py:652

commit v3 on v2

v3 whole, which is shorter than its diff:
```python
import functools
import math

import jax
import jax.numpy as jnp
from jax import lax
from jax.experimental import pallas as pl
from jax.experimental.pallas import tpu as pltpu
from jax.sharding import PartitionSpec as P

MESH = pl.DeviceIdType.MESH
F32 = jnp.float32
BF16 = jnp.bfloat16
PARTS = 2
FEATS = 2
LEADS = (96, 64)


def repeat(steps, step):
    if len(steps) <= 8:
        for d in steps:
            step(d)
    elif len(steps) > 0:

        def one(d, unused):
            step(d)
            return unused

        lax.fori_loop(min(steps), max(steps) + 1, one, 0)


def split_dot(left, right, dims):
    high = left.astype(BF16)
    low = (left - high.astype(F32)).astype(BF16)
    first = lax.dot_general(high, right, dims, preferred_element_type=F32)
    return first + lax.dot_general(low, right, dims, preferred_element_type=F32)


def counts(rows, cols):
    half = cols // 2
    return {
        "load": 5 + FEATS,
        "x_mate": FEATS,
        "x_lead": FEATS,
        "x_rest": FEATS,
        "x_pass": FEATS,
        "yc": PARTS * FEATS * (half // 2),
        "yb": PARTS * (half // 2),
        "rz": PARTS,
        "gz": (1 + FEATS) * (half - 1),
        "gy": 1 + FEATS,
        "c": FEATS,
        "w": 3,
        "s_x": 1,
        "s_ry": 1,
        "s_rz": 1,
        "s_gz": 1,
        "s_gy": 1,
        "s_c": 1,
        "s_w": 3,
    }


EARLY = ("load", "x_mate", "x_lead", "x_rest", "x_pass", "yc", "yb", "rz", "s_x", "s_ry", "s_rz")


def kernel(
    rows,
    cols,
    position_hbm,
    count_hbm,
    x_hbm,
    w_hbm,
    og_hbm,
    values_hbm,
    out_ref,
    ig_ref,
    wg_ref,
    position,
    count,
    values,
    w_ref,
    og_ref,
    xg,
    tile,
    tile_t,
    mate_part,
    mate_in,
    own,
    part,
    part_in,
    keep,
    up,
    acc,
    term_sum,
    term,
    w1_in,
    w2_in,
    w3_in,
    pc,
    pc_in,
    sems,
):
    scope = jax.named_scope
    nodes, width = x_hbm.shape
    slots, block = values_hbm.shape[0], values_hbm.shape[1]
    col_blocks = rows
    my_row = lax.axis_index("row")
    my_col = lax.axis_index("col")
    half = cols // 2
    exts = rows // 2
    high = my_col // 2
    low = lax.rem(my_col, 2)
    mate = high * 2 + 1 - low
    ext = my_row // 2
    core = lax.rem(my_row, 2)
    core_mate = ext * 2 + 1 - core
    plane = 2 * rows
    my_spot = my_row * 2 + low
    sub = nodes // PARTS
    fw = width // FEATS
    leads = [nodes * LEADS[f] // 128 for f in range(FEATS)]
    group = min(half, 4)
    groups = half // group
    wing = half // 2
    side = high // wing
    rank = lax.rem(high, wing)
    ext_steps = list(range(1, exts))
    lead_rows = [pl.ds(0, n) for n in leads]
    rest_rows = [pl.ds(n, nodes - n) for n in leads]

    base, total = {}, {True: 0, False: 0}
    for name, size in counts(rows, cols).items():
        base[name] = total[name in EARLY]
        total[name in EARLY] += size
    arrays = {False: sems}

    def sem(name, index=0):
        return arrays[name in EARLY].at[base[name] + index]

    def across(step):
        def one(j):
            far = (1 - side) * wing + lax.rem(wing - 1 - rank + j, wing)
            step(j, far, far)

        repeat(list(range(wing)), one)

    def beside(step):
        def one(j):
            to = side * wing + lax.rem(rank + j, wing)
            come = side * wing + lax.rem(rank + wing - j, wing)
            step(wing - 1 + j, to, come)

        repeat(list(range(1, wing)), one)

    def far_first(step):
        across(step)
        beside(step)

    def near_first(step):
        beside(step)
        across(step)

    def ext_ahead(d):
        return lax.rem(ext + d, exts)

    def ext_behind(d):
        return lax.rem(ext + exts - d, exts)

    def spot_ahead(d):
        return lax.rem(my_spot + d, plane)

    def move(src, dst, sent, got, **target):
        return pltpu.make_async_remote_copy(
            src_ref=src,
            dst_ref=dst,
            send_sem=sent,
            recv_sem=got,
            device_id=target,
            device_id_type=MESH,
        )

    def arrived(ref, got):
        move(ref, ref, sem("s_c"), got, col=mate).wait_recv()

    def gone(ref, sent):
        move(ref, ref, sent, sem("c"), col=mate).wait_send()

    def repeat_all(count, step):
        if count == 1:
            step(0)
        else:

            def one(g, unused):
                step(g)
                return unused

            lax.fori_loop(0, count, one, 0)

    def to_spots(src, dst, sent, got):
        def one(d):
            spot = spot_ahead(d)
            move(
                src(spot), dst.at[my_spot], sent, got,
                row=spot // 2, col=high * 2 + lax.rem(spot, 2),
            ).start()

        repeat(list(range(1, plane)), one)

    scale = 1.0 / math.sqrt(nodes * rows * cols)
    piece = width // plane
    over_nodes = (((0,), (0,)), ((), ()))
    both = pl.ds(0, FEATS)

    depth = rows * nodes

    def first_half(early):
        arrays[True] = early
        load = pltpu.make_async_copy(values_hbm, values.at[pl.ds(0, slots)], sem("load", 0))
        load_x = [
            pltpu.make_async_copy(
                x_hbm.at[:, pl.ds(f * fw, fw)], xg.at[f, my_row], sem("load", 5 + f)
            )
            for f in range(FEATS)
        ]
        load_w = pltpu.make_async_copy(w_hbm, w_ref, sem("load", 2))
        load_og = pltpu.make_async_copy(og_hbm, og_ref, sem("load", 3))
        load_position = pltpu.make_async_copy(position_hbm, position, sem("load", 4))
        load_count = pltpu.make_async_copy(count_hbm, count, sem("load", 1))
        for one in (*load_x, load_position, load_count, load, load_w, load_og):
            one.start()

        barrier = pltpu.get_barrier_semaphore()

        def greet(**target):
            pl.semaphore_signal(barrier, inc=1, device_id=target, device_id_type=MESH)

        far_first(lambda t, to, come: greet(col=to * 2 + low))

        def greet_spot(d):
            spot = spot_ahead(d)
            greet(row=spot // 2, col=high * 2 + lax.rem(spot, 2))

        repeat(list(range(1, plane)), greet_spot)
        values[slots] = jnp.zeros((block, block), BF16)
        for one in load_x:
            one.wait()
        with scope("bar"):
            pl.semaphore_wait(barrier, plane - 1 + half - 1)

        def x_send(f):
            mine = xg.at[f, my_row]

            def send_lead(d):
                move(
                    mine.at[lead_rows[f]], mine.at[lead_rows[f]], sem("s_x"), sem("x_lead", f),
                    row=ext_ahead(d) * 2 + core,
                ).start()

            def send_rest(d):
                for to in (core, 1 - core):
                    move(
                        mine.at[rest_rows[f]], mine.at[rest_rows[f]], sem("s_x"), sem("x_rest", f),
                        row=ext_ahead(d) * 2 + to,
                    ).start()

            if leads[f] > 0:
                repeat(ext_steps, send_lead)
            move(mine, mine, sem("s_x"), sem("x_mate", f), row=core_mate).start()
            repeat(ext_steps, send_rest)

        for f in range(FEATS):
            x_send(f)

        with scope("load"):
            load_position.wait()
            load_count.wait()
            load.wait()
        live_count = count[0, 0]

        def build(q, y, z, pointer):
            for k in range(col_blocks):
                here = position[jnp.minimum(pointer, slots - 1)]
                live = (here == q * col_blocks + k) & (pointer < live_count)
                value = values[jnp.where(live, pointer, slots)]
                for p in range(PARTS):
                    tile[p, y, z, :, pl.ds(k * block, block)] = value[p * sub : (p + 1) * sub, :]
                pointer = pointer + live.astype(jnp.int32)
            return pointer

        with scope("build"):
            if cols <= 8:
                pointer = jnp.int32(0)
                for q in range(cols):
                    pointer = build(q, q % 2, q // 2, pointer)
            else:

                def build_pair(z, pointer):
                    for y in range(2):
                        pointer = build(z * 2 + y, y, z, pointer)
                    return pointer

                lax.fori_loop(0, half, build_pair, jnp.int32(0))

        def x_relay(f):
            if leads[f] == 0:
                return
            with scope("x_lead%d" % f):
                arrived(xg.at[f, pl.ds(0, exts - 1), lead_rows[f]], sem("x_lead", f))

            def one(d):
                slot = xg.at[f, ext_behind(d) * 2 + core, lead_rows[f]]
                move(slot, slot, sem("s_x"), sem("x_pass", f), row=core_mate).start()

            repeat(ext_steps, one)

        def x_wait(f):
            with scope("x_rest%d" % f):
                arrived(xg.at[f, 0], sem("x_mate", f))
                arrived(xg.at[f, pl.ds(0, 2 * (exts - 1)), rest_rows[f]], sem("x_rest", f))
            if leads[f] == 0:
                return
            with scope("x_pass%d" % f):
                arrived(xg.at[f, pl.ds(0, exts - 1), lead_rows[f]], sem("x_pass", f))

        def product(p, f, y, g):
            left = tile[p, y, pl.ds(g * group, group)].reshape(group * sub, depth)
            panel = xg[f].reshape(depth, fw)
            return jnp.dot(left, panel, preferred_element_type=F32).reshape(group, sub, fw)

        def yc(p, f, j):
            return sem("yc", (p * FEATS + f) * wing + j)

        def yb(p, j):
            return sem("yb", p * wing + j)

        def for_mate(p, f):
            def one(g):
                mate_part[p, f, pl.ds(g * group, group)] = product(p, f, 1 - low, g).astype(BF16)

            repeat_all(groups, one)

            def send(j, z, unused):
                move(
                    mate_part.at[p, f, z], mate_in.at[p, f, z], sem("s_ry"), yc(p, f, j), col=mate
                ).start()

            across(send)

        def for_mate_near(p):
            def send(t, z, unused):
                move(
                    mate_part.at[p, :, z], mate_in.at[p, :, z], sem("s_ry"), yb(p, t - wing), col=mate
                ).start()

            beside(send)
            send(2 * wing - 1, high, high)

        def for_me(p, f):
            def one(g):
                own[p, f, pl.ds(g * group, group)] = product(p, f, low, g)

            repeat_all(groups, one)

        x_relay(0)
        x_wait(0)
        with scope("fwd0"):
            for_mate(0, 0)
        for f in range(1, FEATS):
            x_relay(f)
        for f in range(1, FEATS):
            x_wait(f)
            for_mate(0, f)
        with scope("fwd1"):
            for p in range(1, PARTS):
                for f in range(FEATS):
                    for_mate(p, f)
            for p in range(PARTS):
                for_mate_near(p)
            for p in range(PARTS):
                for f in range(FEATS):
                    for_me(p, f)

        def turn(p, y):
            def one(g):
                for k in range(col_blocks):
                    left = tile[p, y, pl.ds(g * group, group), :, pl.ds(k * block, block)]
                    tile_t[p, y, g, pl.ds(k * block, block), :] = left.reshape(group * sub, block).T

            repeat_all(groups, one)

        with scope("turn"):
            for p in range(PARTS):
                for y in range(2):
                    turn(p, y)

        def to_across(p, f):
            def one(j, z, unused):
                arrived(mate_in.at[p, f, z], yc(p, f, j))
                part[p, f, z] = (own[p, f, z] + mate_in[p, f, z].astype(F32)).astype(BF16)
                move(
                    part.at[p, f, z], part_in.at[p, f, high], sem("s_rz"), sem("rz", p),
                    col=z * 2 + low,
                ).start()

            across(one)

        def to_beside(p):
            def one(t, z, unused):
                arrived(mate_in.at[p, :, z], yb(p, t - wing))
                part[p, :, z] = (own[p, :, z] + mate_in[p, :, z].astype(F32)).astype(BF16)
                move(
                    part.at[p, :, z], part_in.at[p, :, high], sem("s_rz"), sem("rz", p),
                    col=z * 2 + low,
                ).start()

            beside(one)
            arrived(mate_in.at[p, :, high], yb(p, wing - 1))
            keep[p] = own[p, :, high] + mate_in[p, :, high].astype(F32)

        for p in range(PARTS):
            for f in range(FEATS):
                with scope("across%d%d" % (p, f)):
                    to_across(p, f)
        for p in range(PARTS):
            with scope("beside%d" % p):
                to_beside(p)

        load_w.wait()
        load_og.wait()
        def spread(f, p, index):
            mine = up.at[f, p, low, high]
            far_first(
                lambda t, z, unused: move(
                    mine, mine, sem("s_gz"), sem("gz", index * (half - 1) + t), col=z * 2 + low
                ).start()
            )
            move(mine, mine, sem("s_gy"), sem("gy", index), col=mate).start()

        def middle(p):
            with scope("rz%d" % p):
                arrived(part_in.at[p, :, pl.ds(0, half - 1)], sem("rz", p))

            def add(t, unused, z):
                keep[p] += part_in[p, :, z].astype(F32)

            near_first(add)
            mixed = jnp.concatenate([keep[p, f] for f in range(FEATS)], axis=1)
            pre = split_dot(mixed, w_ref[...], (((1,), (0,)), ((), ())))
            decay = jnp.exp(jnp.minimum(pre, 0.0))
            slope = jnp.where(pre > 0, 1.0, decay)
            some = pl.ds(p * sub, sub)
            upstream = (og_ref[some].astype(F32) * slope).astype(BF16)
            for f in range(FEATS):
                up[f, p, low, high] = upstream[:, f * fw : (f + 1) * fw]
            if p < PARTS - 1:
                spread(both, p, 0)
            else:
                for f in range(FEATS):
                    spread(f, p, 1 + f)
            out_ref[some] = jnp.where(pre > 0, pre, decay - 1.0).astype(BF16)
            share = split_dot(mixed, upstream, over_nodes)
            if p == 0:
                term_sum[...] = share
            else:
                share = term_sum[...] + share
                term[...] = (share * scale).reshape(plane, piece, width).astype(BF16)

        for p in range(PARTS):
            with scope("middle%d" % p):
                middle(p)

        with scope("w1_send"):
            to_spots(lambda spot: term.at[spot], w1_in, sem("s_w", 0), sem("w", 0))
            w1_in[my_spot] = term[my_spot]
        with scope("gone_early"):
            gone(xg.at[:, pl.ds(0, rows - 1)], sem("s_x"))
            gone(mate_part, sem("s_ry"))
            gone(part.at[:, :, pl.ds(0, half - 1)], sem("s_rz"))

    pl.run_scoped(first_half, pltpu.SemaphoreType.DMA((total[True],)))

    def region(f, p, z):
        return up.at[f, p, low, z]

    def pass_on(f, p, index):
        def one(t, unused, z):
            slot = region(f, p, z)
            arrived(slot, sem("gz", index * (half - 1) + t))
            move(slot, slot, sem("s_gy"), sem("gy", index), col=mate).start()

        near_first(one)

    def back(f, p, y, first=False):
        def one(g):
            right = up[f, p, y, pl.ds(g * group, group)].reshape(group * sub, fw)
            got = jnp.dot(tile_t[p, y, g], right, preferred_element_type=F32)
            if first:
                acc[f] = got
            else:
                acc[f] += got

        if first and groups > 1:
            acc[f] = jnp.zeros(acc.shape[1:], F32)
            first = False
        repeat_all(groups, one)

    with scope("gz_p0"):
        pass_on(both, 0, 0)
    for f in range(FEATS):
        back(f, 0, low, first=True)
    for f in range(FEATS):
        with scope("gz_p1_%d" % f):
            pass_on(f, 1, 1 + f)
    with scope("w1_wait"):
        arrived(w1_in.at[pl.ds(0, plane - 1)], sem("w", 0))
        w2_in[high] = jnp.sum(w1_in[...].astype(F32), axis=0).astype(BF16)
        far_first(
            lambda t, z, unused: move(
                w2_in.at[high], w2_in.at[high], sem("s_w", 1), sem("w", 1), col=z * 2 + low
            ).start()
        )
    for f in range(FEATS):
        back(f, 1, low)

    with scope("gy_p0"):
        arrived(up.at[both, 0, 1 - low], sem("gy", 0))
    for f in range(FEATS):
        back(f, 0, 1 - low)

    def block_of(r):
        return pl.ds(pl.multiple_of(r * nodes, nodes), nodes)

    def launch(f):
        def one(r):
            pc[f, r] = acc[f, block_of(r)].astype(BF16)
            move(pc.at[f, r], pc_in.at[f, my_row], sem("s_c"), sem("c", f), row=r).start()

        def outside(d):
            one(ext_ahead(d) * 2 + core)
            one(ext_ahead(d) * 2 + 1 - core)

        repeat(ext_steps, outside)
        one(core_mate)

    def gather_grad(f):
        arrived(pc_in.at[f, pl.ds(0, rows - 1)], sem("c", f))

        def add(r):
            acc[f, block_of(my_row)] += pc_in[f, r].astype(F32)

        def outside(d):
            for k in range(2):
                add(ext_behind(d) * 2 + k)

        repeat(ext_steps, outside)
        add(core_mate)
        some = pl.ds(f * fw, fw)
        return split_dot(acc[f, block_of(my_row)], w_ref[:, some], (((1,), (1,)), ((), ())))

    for f in range(FEATS):
        with scope("gy_p1_%d" % f):
            arrived(up.at[f, 1, 1 - low], sem("gy", 1 + f))
        back(f, 1, 1 - low)
        with scope("launch%d" % f):
            launch(f)
    with scope("w2_wait"):
        arrived(w2_in.at[pl.ds(0, half - 1)], sem("w", 1))
        w3_in[my_spot] = jnp.sum(w2_in[...].astype(F32), axis=0).astype(BF16)
        to_spots(lambda spot: w3_in.at[my_spot], w3_in, sem("s_w", 2), sem("w", 2))
    grad = 0.0
    for f in range(FEATS):
        with scope("grad%d" % f):
            grad = grad + gather_grad(f)
    ig_ref[...] = grad.astype(BF16)

    with scope("gone"):
        gone(up.at[:, :, low, pl.ds(0, half - 1)], sem("s_gz"))
        gone(up.at[:, :, low], sem("s_gy"))
        gone(pc.at[:, pl.ds(0, rows - 1)], sem("s_c"))
        gone(term.at[pl.ds(0, plane - 1)], sem("s_w", 0))
        gone(w2_in.at[pl.ds(0, half - 1)], sem("s_w", 1))
        gone(w3_in.at[pl.ds(0, plane - 1)], sem("s_w", 2))
    with scope("w3_wait"):
        arrived(w3_in.at[pl.ds(0, plane - 1)], sem("w", 2))
    wg_ref[...] = w3_in[...].reshape(width, width).astype(F32)


def finish(out_ref, ig_ref, wg_ref, out_hbm, ig_hbm, wg_hbm, sem):
    trio = ((out_ref, out_hbm), (ig_ref, ig_hbm), (wg_ref, wg_hbm))
    copies = [pltpu.make_async_copy(a, b, sem.at[i]) for i, (a, b) in enumerate(trio)]
    for copy in copies:
        copy.start()
    for copy in copies:
        copy.wait()


def body(node_features, layer_weight, output_grad, block_values, block_position, tile_count):
    rows, cols = lax.axis_size("row"), lax.axis_size("col")
    nodes, width = node_features.shape
    slots, block = block_values.shape[2], block_values.shape[3]
    half, exts, plane = cols // 2, rows // 2, 2 * rows
    assert nodes == block and cols == 2 * half and rows == 2 * exts
    sub, fw = nodes // PARTS, width // FEATS
    group = min(half, 4)
    groups = half // group
    piece = width // plane
    depth = rows * nodes
    place = pl.BlockSpec(memory_space=pl.ANY)
    pinned = pl.BlockSpec(memory_space=pltpu.HBM)
    inside = pl.BlockSpec(memory_space=pltpu.VMEM)
    dma = pltpu.SemaphoreType.DMA
    vmem = pltpu.VMEM
    shapes = (
        jax.ShapeDtypeStruct((nodes, width), BF16),
        jax.ShapeDtypeStruct((nodes, width), BF16),
        jax.ShapeDtypeStruct((width, width), F32),
    )
    results = pl.pallas_call(
        functools.partial(kernel, rows, cols),
        out_shape=(
            vmem((nodes, width), BF16),
            vmem((nodes, width), BF16),
            vmem((width, width), F32),
        ),
        in_specs=[pinned, pinned, place, place, place, place],
        out_specs=(inside, inside, inside),
        scratch_shapes=[
            pltpu.SMEM((slots,), jnp.int32),
            pltpu.SMEM((1, 1), jnp.int32),
            vmem((slots + 1, block, block), BF16),
            vmem((width, width), BF16),
            vmem((nodes, width), BF16),
            vmem((FEATS, rows, nodes, fw), BF16),
            vmem((PARTS, 2, half, sub, depth), BF16),
            vmem((PARTS, 2, groups, depth, group * sub), BF16),
            vmem((PARTS, FEATS, half, sub, fw), BF16),
            vmem((PARTS, FEATS, half, sub, fw), BF16),
            vmem((PARTS, FEATS, half, sub, fw), F32),
            vmem((PARTS, FEATS, half, sub, fw), BF16),
            vmem((PARTS, FEATS, half, sub, fw), BF16),
            vmem((PARTS, FEATS, sub, fw), F32),
            vmem((FEATS, PARTS, 2, half, sub, fw), BF16),
            vmem((FEATS, depth, fw), F32),
            vmem((width, width), F32),
            vmem((plane, piece, width), BF16),
            vmem((plane, piece, width), BF16),
            vmem((half, piece, width), BF16),
            vmem((plane, piece, width), BF16),
            vmem((FEATS, rows, nodes, fw), BF16),
            vmem((FEATS, rows, nodes, fw), BF16),
            dma((sum(n for name, n in counts(rows, cols).items() if name not in EARLY),)),
        ],
        compiler_params=pltpu.CompilerParams(collective_id=0, has_side_effects=True),
    )(
        block_position.reshape(slots),
        tile_count,
        node_features,
        layer_weight,
        output_grad,
        block_values.reshape(slots, block, block),
    )
    return pl.pallas_call(
        finish,
        out_shape=shapes,
        in_specs=[inside] * 3,
        out_specs=(place,) * 3,
        scratch_shapes=[
            dma((3,)),
        ],
        compiler_params=pltpu.CompilerParams(vmem_limit_bytes=4 << 20),
    )(*results)


def solution(mesh):
    in_specs = (
        P(("row", "col"), None),
        P(),
        P(("row", "col"), None),
        P("row", "col", None, None, None),
        P("row", "col", None),
        P("row", "col"),
    )
    out_specs = (P(("row", "col"), None), P(("row", "col"), None), P())
    return jax.shard_map(body, mesh=mesh, in_specs=in_specs, out_specs=out_specs, check_vma=False)
```

time: 35.3 us -> 34.9 us (0.989)
  Pallas kernels: 33.9 us -> 33.5 us
    pallas_call x1, Pallas kernels: 33.1 us -> 32.7 us  [body(): pl.pallas_call(functools.partial(kernel, rows, cols), out_shape=(vmem((no...]
where the time goes in v3:
time: 34.9 us; the launch traced here: 34.7 us
  Pallas kernels  33.5 us (96%)
  between operations  1.29 us (4%)
    pallas_call x1, Pallas kernels, body(): pl.pallas_call(functools.partial(kernel, rows, cols), out_shape=(vmem((no...  32.7 us
    pallas_call x1, Pallas kernels, body(): pl.pallas_call(finish, out_shape=shapes, in_specs=[inside] * 3, out_specs...  0.77 us

profile of v3, /device:TPU:0, one launch (start us, length us, event | category | flops | bytes accessed | tf_op | source)
XLA Modules:
  0.0 34.7 jit_solution(3243163388396982099)
XLA Ops:
  1.3 32.7 %shard_map.85 = (bf16[128,256]{1,0:T(8,128)(2,1)S(1)}, bf16[128,256]{1,0:T(8,128)(2,1)S(1)}, f32[256,256]{1,0:T(8,128)S(1)}) custom-call(s32[24]{0:T(128)} %bitcast.3, s32[1,1]{1,0:T(1,128)S(6)} %copy.9.count_hbm, bf16[128,256]{1,0:T(8,128)(2,1)} %x_hbm.1, bf16[256,256]{1,0:T(8,128)(2,1)} %w_hbm.1, bf16[128,256]{1,0:T(8,128)(2,1)} %og_hbm.1, ...), custom_call_target="tpu_custom_call" | custom-call | tf_op jit(solution)/shard_map/pallas_call | solution.py:619
  34.0 0.8 %shard_map.86 = (bf16[128,256]{1,0:T(8,128)(2,1)}, bf16[128,256]{1,0:T(8,128)(2,1)}, f32[256,256]{1,0:T(8,128)}) custom-call(bf16[128,256]{1,0:T(8,128)(2,1)S(1)} %get-tuple-element.6.out_ref, bf16[128,256]{1,0:T(8,128)(2,1)S(1)} %get-tuple-element.7.ig_ref, f32[256,256]{1,0:T(8,128)S(1)} %get-tuple-element.8.wg_ref), custom_call_target="tpu_custom_call" | custom-call | tf_op jit(solution)/shard_map/pallas_call | solution.py:663
